TPU v7x, 32 devices: a whole 2x2x4 slice. The times are simulated.
32 devices in a mesh: row: 4 (over y, core), col: 8 (over z, x).
Axes of the slice: x: 2, y: 2, z: 4, core: 2. Of those that a mesh axis runs over, the one named last changes fastest.
Arguments:
- fock: float32 [2, 8192, 8192], P(None, 'row', 'col'), may hold values from -1.1875 to 1.1875, as said below
- density: float32 [2, 8192, 8192], P(None, 'row', 'col'), may hold values from -1.09375 to 1.09375, as said below
- probe: float32 [2, 8192, 128], P(None, 'col'), may hold values from -6 to 6
Outputs:
- propagated: float32 [2, 8192, 128], P(None, 'col')
Inputs may be any that keep to these rules, and one draw needn't show every extreme that they name: Hermitian: fock[0] is symmetric and fock[1] antisymmetric, exactly. Hermitian: density[0] is symmetric and density[1] antisymmetric, exactly.
All inputs are finite; a program needn't handle non-finite values.
Results may differ from a plain program's by a relative error of at most 0.00011.
Values sent between devices are 32-bit elements; how exact they have to be, the bound alone decides.
A program may use at most 128 MiB of HBM per device.

v0:
```python
import jax
import jax.numpy as jnp
from jax import lax
from jax.sharding import PartitionSpec as P

time_step = 0.5


def broadcast(block, axis, owner):
    block = jnp.where(lax.axis_index(axis) == owner, block, jnp.zeros_like(block))
    return lax.psum(block, axis)


def plain_dot(left, right):
    return jnp.dot(left, right, precision=lax.Precision.HIGHEST, preferred_element_type=jnp.float32)


def adjoint_dot(left, right):
    return lax.dot_general(
        left,
        right,
        (((0,), (0,)), ((), ())),
        precision=lax.Precision.HIGHEST,
        preferred_element_type=jnp.float32,
    )


def prepare(matrix, adjoint):
    real_m = matrix[0]
    imag_m = -matrix[1] if adjoint else matrix[1]
    return (real_m, imag_m, real_m + imag_m, imag_m - real_m)


def complex_product(pieces, vector, adjoint):
    multiply = adjoint_dot if adjoint else plain_dot
    real_m, imag_m, sum_m, diff_m = pieces
    real_v = vector[0]
    imag_v = vector[1]
    real_part = multiply(real_m, real_v) - multiply(imag_m, imag_v)
    imag_part = multiply(real_m, imag_v) + multiply(imag_m, real_v)
    return jnp.stack([real_part, imag_part])


def times_imag(vector, factor):
    return jnp.stack([-factor * vector[1], factor * vector[0]])


def shards(fock, density, probe):
    rows_block = fock.shape[1]
    cols_block = fock.shape[2]
    fock_plain = prepare(fock, False)
    fock_adjoint = prepare(fock, True)
    density_plain = prepare(density, False)

    def reduce_cols(partial_value):
        share = lax.psum_scatter(partial_value, "col", scatter_dimension=1, tiled=True)
        return lax.all_gather(share, "col", axis=1, tiled=True)

    def to_columns(vector):
        column = lax.axis_index("col")
        source = column * cols_block // rows_block
        offset = column * cols_block - source * rows_block
        piece = lax.dynamic_slice_in_dim(vector, offset, cols_block, 1)
        return broadcast(piece, "row", source)

    def forward(pieces, vector):
        return reduce_cols(complex_product(pieces, vector, False))

    def backward(pieces, vector):
        return lax.psum(complex_product(pieces, vector, True), "row")

    def alternate(vector, in_columns, sign):
        current = vector
        column_sum = vector if in_columns else None
        row_sum = None if in_columns else vector
        if in_columns:
            current = forward(fock_plain, current)
        else:
            current = backward(fock_adjoint, current)
        in_columns = not in_columns
        current = times_imag(current, sign * time_step / 1)
        if in_columns:
            column_sum = current
        else:
            row_sum = current
        return (column_sum, row_sum)

    column_sum, row_sum = alternate(probe, True, 1.0)
    first = column_sum + to_columns(row_sum)
    second = forward(density_plain, first)
    column_sum, row_sum = alternate(second, False, -1.0)
    result = column_sum + to_columns(row_sum)
    return result


def solution(mesh):
    return jax.shard_map(
        shards,
        mesh=mesh,
        in_specs=(P(None, "row", "col"), P(None, "row", "col"), P(None, "col", None)),
        out_specs=P(None, "col", None),
        check_vma=False,
    )
```

profile of v0, /device:TPU:15, one launch (start us, length us, event | category | flops | bytes accessed | tf_op | source)
XLA Modules:
  0.0 481.3 jit_solution(5224947570114361618)
XLA Ops:
  6.5 9.3 %fusion.12 = f32[2048,128]{1,0:T(8,128)S(1)} fusion(f32[2,2048,1024]{2,1,0:T(8,128)} %param.3, f32[2,1024,128]{2,1,0:T(8,128)} %param.5), kind=kOutput, calls=%fused_computation.12 | convolution fusion | flops 3221225472 | bytes 9961472 | tf_op jit(solution)/shard_map/dot_general | solution.py:15
  15.9 9.2 %fusion.14 = f32[2048,128]{1,0:T(8,128)S(1)} fusion(f32[2,2048,1024]{2,1,0:T(8,128)} %param.3, f32[2,1024,128]{2,1,0:T(8,128)S(1)} %copy-done.2), kind=kOutput, calls=%fused_computation.14 | convolution fusion | flops 3221225472 | bytes 9961472 | tf_op jit(solution)/shard_map/dot_general | solution.py:15
  25.1 7.0 %fusion.47 = f32[1,2048,128]{2,1,0:T(8,128)S(1)} fusion(f32[2048,128]{1,0:T(8,128)S(1)} %fusion.12, f32[2,2048,1024]{2,1,0:T(8,128)S(1)} %copy-done, f32[2,1024,128]{2,1,0:T(8,128)S(1)} %copy-done.2), kind=kOutput, calls=%fused_computation.41 | convolution fusion | flops 3221487616 | bytes 11010048 | tf_op jit(solution)/shard_map/dot_general | solution.py:15
  32.1 7.3 %fusion.41 = f32[1,2048,128]{2,1,0:T(8,128)S(1)} fusion(f32[2048,128]{1,0:T(8,128)S(1)} %fusion.14, f32[2,2048,1024]{2,1,0:T(8,128)S(1)} %copy-done, f32[2,1024,128]{2,1,0:T(8,128)S(1)} %copy-done.2), kind=kOutput, calls=%fused_computation.39 | convolution fusion | flops 3221487616 | bytes 11010048 | tf_op jit(solution)/shard_map/dot_general | solution.py:15
  39.4 1.5 pad_maximum_fusion
  41.0 67.4 %reduce-scatter.3.cloned.1.call-done = f32[2,256,128]{2,1,0:T(8,128)} async-done(((f32[2,2048,128]{2,1,0:T(8,128)}), f32[2,256,128]{2,1,0:T(8,128)}) %reduce-scatter.3.cloned.1.call-update) | async-done | bytes 262160 | tf_op jit(solution)/shard_map/reduce_scatter | solution.py:56
  108.5 50.2 %all-gather.3.cloned.1.call-done = f32[2,2048,128]{2,1,0:T(8,128)} async-done(((f32[2,256,128]{2,1,0:T(8,128)}), f32[2,2048,128]{2,1,0:T(8,128)}) %all-gather.3.cloned.1.call-update) | async-done | bytes 2097168 | tf_op jit(solution)/shard_map/all_gather | solution.py:57
  158.7 1.7 slice_multiply_fusion
  161.5 36.3 %all-reduce.4.cloned.1.call-done = f32[2,1024,128]{2,1,0:T(8,128)} async-done(((f32[2,1024,128]{2,1,0:T(8,128)}), f32[2,1024,128]{2,1,0:T(8,128)}) %all-reduce.4.cloned.1.call-update) | async-done | bytes 1048592 | tf_op jit(solution)/shard_map/psum | solution.py:11
  197.8 1.3 add.38
  199.1 9.2 %fusion.4 = f32[128,2048]{0,1:T(8,128)S(1)} fusion(f32[2,2048,1024]{2,1,0:T(8,128)} %param.4, f32[2,1024,128]{2,1,0:T(8,128)S(1)} %add.38), kind=kOutput, calls=%fused_computation.4 | convolution fusion | flops 3221225472 | bytes 9961472 | tf_op jit(solution)/shard_map/dot_general | solution.py:15
  208.4 10.0 %fusion.6 = f32[128,2048]{0,1:T(8,128)S(1)} fusion(f32[2,2048,1024]{2,1,0:T(8,128)} %param.4, f32[2,1024,128]{2,1,0:T(8,128)S(1)} %add.38), kind=kOutput, calls=%fused_computation.6 | convolution fusion | flops 3221225472 | bytes 9961472 | tf_op jit(solution)/shard_map/dot_general | solution.py:15
  218.4 9.7 %fusion.59 = f32[1,2048,128]{2,1,0:T(8,128)S(1)} fusion(f32[128,2048]{0,1:T(8,128)S(1)} %fusion.4, f32[2,2048,1024]{2,1,0:T(8,128)} %param.4, f32[2,1024,128]{2,1,0:T(8,128)S(1)} %add.38), kind=kOutput, calls=%fused_computation.45 | convolution fusion | flops 3221487616 | bytes 11010048 | tf_op jit(solution)/shard_map/dot_general | solution.py:15
  228.2 7.1 %fusion.53 = f32[1,2048,128]{2,1,0:T(8,128)S(1)} fusion(f32[128,2048]{0,1:T(8,128)S(1)} %fusion.6, f32[2,2048,1024]{2,1,0:T(8,128)S(1)} %bitcast.102, f32[2,1024,128]{2,1,0:T(8,128)S(1)} %add.38), kind=kOutput, calls=%fused_computation.43 | convolution fusion | flops 3221487616 | bytes 11010048 | tf_op jit(solution)/shard_map/dot_general | solution.py:15
  235.3 1.5 pad_maximum_fusion.1
  236.9 67.7 %reduce-scatter.5.cloned.1.call-done = f32[2,256,128]{2,1,0:T(8,128)} async-done(((f32[2,2048,128]{2,1,0:T(8,128)}), f32[2,256,128]{2,1,0:T(8,128)}) %reduce-scatter.5.cloned.1.call-update) | async-done | bytes 262160 | tf_op jit(solution)/shard_map/reduce_scatter | solution.py:56
  304.7 50.1 %all-gather.5.cloned.1.call-done = f32[2,2048,128]{2,1,0:T(8,128)} async-done(((f32[2,256,128]{2,1,0:T(8,128)}), f32[2,2048,128]{2,1,0:T(8,128)}) %all-gather.5.cloned.1.call-update) | async-done | bytes 2097168 | tf_op jit(solution)/shard_map/all_gather | solution.py:57
  354.8 16.0 %fusion = f32[128,1024]{0,1:T(8,128)S(1)} fusion(f32[2,2048,1024]{2,1,0:T(8,128)} %param.3, f32[2,2048,128]{2,1,0:T(8,128)} %all-gather.5.cloned.1.call-done), kind=kOutput, calls=%fused_computation | convolution fusion | flops 3223322624 | bytes 9961472 | tf_op jit(solution)/shard_map/dot_general | solution.py:19
  370.8 17.0 %fusion.2 = f32[128,1024]{0,1:T(8,128)S(1)} fusion(f32[2,2048,1024]{2,1,0:T(8,128)} %param.3, f32[2,2048,128]{2,1,0:T(8,128)} %all-gather.5.cloned.1.call-done), kind=kOutput, calls=%fused_computation.2 | convolution fusion | flops 3223322624 | bytes 9961472 | tf_op jit(solution)/shard_map/dot_general | solution.py:19
  387.9 16.4 %fusion.68 = f32[1,1024,128]{2,1,0:T(8,128)S(1)} fusion(f32[128,1024]{0,1:T(8,128)S(1)} %fusion, f32[2,2048,1024]{2,1,0:T(8,128)} %param.3, f32[2,2048,128]{2,1,0:T(8,128)S(1)} %copy-done.1), kind=kOutput, calls=%fused_computation.52 | convolution fusion | flops 3221356544 | bytes 10485760 | tf_op jit(solution)/shard_map/dot_general | solution.py:19
  404.4 13.4 %fusion.71 = f32[1,1024,128]{2,1,0:T(8,128)S(1)} fusion(f32[128,1024]{0,1:T(8,128)S(1)} %fusion.2, f32[2,2048,1024]{2,1,0:T(8,128)S(1)} %bitcast.100, f32[2,2048,128]{2,1,0:T(8,128)S(1)} %copy-done.1), kind=kOutput, calls=%fused_computation.53 | convolution fusion | flops 3221356544 | bytes 10485760 | tf_op jit(solution)/shard_map/dot_general | solution.py:19
  417.8 1.5 pad_maximum_fusion.2
  419.3 51.1 %all-reduce.6.cloned.1.call-done = (f32[2,1024,128]{2,1,0:T(8,128)}, f32[2,1024,128]{2,1,0:T(8,128)}) async-done(((f32[2,1024,128]{2,1,0:T(8,128)}, f32[2,1024,128]{2,1,0:T(8,128)}), (f32[2,1024,128]{2,1,0:T(8,128)}, f32[2,1024,128]{2,1,0:T(8,128)})) %all-reduce.6.cloned.1.call-update) | async-done | bytes 2097168 | tf_op jit(solution)/shard_map/psum | solution.py:11
  471.7 2.3 maximum_add_fusion
  (38 shorter events, 2.7 us)
Async XLA Ops:
  6.5 9.3 %copy-start.2 = (f32[2,1024,128]{2,1,0:T(8,128)S(1)}, f32[2,1024,128]{2,1,0:T(8,128)}, u32[]{:S(2)}) copy-start(f32[2,1024,128]{2,1,0:T(8,128)} %param.5) | copy-start | bytes 3145732
  6.5 101.8 %reduce-scatter.3.cloned.1.call-start = ((), (), s32[]{:S(2)}) async-start(), calls=%async_computation.2 | async-start | bytes 2359296 | tf_op jit(solution)/shard_map/reduce_scatter | solution.py:56
  6.5 18.6 %copy-start = (f32[2,2048,1024]{2,1,0:T(8,128)S(1)}, f32[2,2048,1024]{2,1,0:T(8,128)}, u32[]{:S(2)}) copy-start(f32[2,2048,1024]{2,1,0:T(8,128)} %param.3) | copy-start | bytes 50331652
  40.9 117.8 %all-gather.3.cloned.1.call-start = ((), (), s32[]{:S(2)}) async-start(), calls=%async_computation.3 | async-start | bytes 2359296 | tf_op jit(solution)/shard_map/all_gather | solution.py:57
  108.4 89.4 %all-reduce.4.cloned.1.call-start = ((), (), s32[]{:S(2)}) async-start(), calls=%async_computation.4 | async-start | bytes 2097152 | tf_op jit(solution)/shard_map/psum | solution.py:11
  161.5 143.1 %reduce-scatter.5.cloned.1.call-start = ((), (), s32[]{:S(2)}) async-start(), calls=%async_computation.5 | async-start | bytes 2359296 | tf_op jit(solution)/shard_map/reduce_scatter | solution.py:56
  199.1 29.0 %slice-start.4 = ((s8[16777216]{0:T(1024)(128)(4,1)}), s8[4194304]{0:T(1024)(128)(4,1)S(1)}, s32[]{:S(2)}) async-start(s8[16777216]{0:T(1024)(128)(4,1)} %bitcast.101), calls=%async_computation.12 | async-start | bytes 8388608
  199.1 29.0 %slice-start.5 = ((s8[16777216]{0:T(1024)(128)(4,1)}), s8[4194304]{0:T(1024)(128)(4,1)S(1)}, s32[]{:S(2)}) async-start(s8[16777216]{0:T(1024)(128)(4,1)} %bitcast.101), calls=%async_computation.13 | async-start | bytes 8388608
  208.4 19.8 %slice-start.6 = ((s8[16777216]{0:T(1024)(128)(4,1)}), s8[4194304]{0:T(1024)(128)(4,1)S(1)}, s32[]{:S(2)}) async-start(s8[16777216]{0:T(1024)(128)(4,1)} %bitcast.101), calls=%async_computation.14 | async-start | bytes 8388608
  218.4 9.8 %slice-start.7 = ((s8[16777216]{0:T(1024)(128)(4,1)}), s8[4194304]{0:T(1024)(128)(4,1)S(1)}, s32[]{:S(2)}) async-start(s8[16777216]{0:T(1024)(128)(4,1)} %bitcast.101), calls=%async_computation.15 | async-start | bytes 8388608
  236.8 117.9 %all-gather.5.cloned.1.call-start = ((), (), s32[]{:S(2)}) async-start(), calls=%async_computation.6 | async-start | bytes 2359296 | tf_op jit(solution)/shard_map/all_gather | solution.py:57
  304.6 165.8 %all-reduce.6.cloned.1.call-start = ((), (), s32[]{:S(2)}) async-start(), calls=%async_computation.7 | async-start | bytes 4194304 | tf_op jit(solution)/shard_map/psum | solution.py:11
  354.8 33.1 %copy-start.1 = (f32[2,2048,128]{2,1,0:T(8,128)S(1)}, f32[2,2048,128]{2,1,0:T(8,128)}, u32[]{:S(2)}) copy-start(f32[2,2048,128]{2,1,0:T(8,128)} %all-gather.5.cloned.1.call-done) | copy-start | bytes 6291460
  354.8 49.5 %slice-start = ((s8[16777216]{0:T(1024)(128)(4,1)}), s8[4194304]{0:T(1024)(128)(4,1)S(1)}, s32[]{:S(2)}) async-start(s8[16777216]{0:T(1024)(128)(4,1)} %bitcast.99), calls=%async_computation.8 | async-start | bytes 8388608
  354.8 49.6 %slice-start.1 = ((s8[16777216]{0:T(1024)(128)(4,1)}), s8[4194304]{0:T(1024)(128)(4,1)S(1)}, s32[]{:S(2)}) async-start(s8[16777216]{0:T(1024)(128)(4,1)} %bitcast.99), calls=%async_computation.9 | async-start | bytes 8388608
  370.8 33.5 %slice-start.2 = ((s8[16777216]{0:T(1024)(128)(4,1)}), s8[4194304]{0:T(1024)(128)(4,1)S(1)}, s32[]{:S(2)}) async-start(s8[16777216]{0:T(1024)(128)(4,1)} %bitcast.99), calls=%async_computation.10 | async-start | bytes 8388608
  387.9 16.5 %slice-start.3 = ((s8[16777216]{0:T(1024)(128)(4,1)}), s8[4194304]{0:T(1024)(128)(4,1)S(1)}, s32[]{:S(2)}) async-start(s8[16777216]{0:T(1024)(128)(4,1)} %bitcast.99), calls=%async_computation.11 | async-start | bytes 8388608
Sparse Core Ops, SparseCore 0:
  41.0 67.2 reduce-scatter.2
  110.6 48.1 all-gather.2
  161.6 36.1 all-reduce.3
  237.0 67.5 reduce-scatter.4
  306.6 48.0 all-gather.4
  419.4 50.9 all-reduce.5
where the time goes:
time: 490 us; the launch traced here: 481 us
  waiting for transfers between devices  323 us (66%)
  matrix products  132 us (27%)
  between operations  14.2 us (3%)
  other arithmetic  12.1 us (2%)
    reduce_scatter x2, waiting for transfers between devices, reduce_cols(): lax.psum_scatter(partial_value, 'col', scatter_dimension=1, tiled=True)  135 us
    all_gather x2, waiting for transfers between devices, reduce_cols(): return lax.all_gather(share, 'col', axis=1, tiled=True)  100 us
    psum x2, waiting for transfers between devices, broadcast(): return lax.psum(block, axis)  87.4 us
    dot_general x8, matrix products, plain_dot(): jnp.dot(left, right, precision=lax.Precision.HIGHEST, preferred_element_t...  68.9 us
    dot_general x4, matrix products, adjoint_dot(): lax.dot_general(left, right, (((0,), (0,)), ((), ())), precision=lax.Prec...  62.9 us
  transfers between devices with their start and end apart: 6, of which 6 were waited for; matrix products, arithmetic and copies ran while one was open for 0% of the time, Pallas kernels for 0%

commit v1 on v0

v1 whole, which is shorter than its diff:
```python
import functools

import jax
import jax.numpy as jnp
from jax import lax
from jax.experimental import pallas as pl
from jax.experimental.pallas import tpu as pltpu
from jax.sharding import PartitionSpec as P

time_step = 0.5
MESH = pl.DeviceIdType.MESH


def split(value):
    high = value.astype(jnp.bfloat16)
    return high, (value - high.astype(jnp.float32)).astype(jnp.bfloat16)


def dot3(left, right):
    dot = functools.partial(jnp.dot, preferred_element_type=jnp.float32)
    return dot(left[0], right[0]) + (dot(left[0], right[1]) + dot(left[1], right[0]))


def kernel(
    nr, nc, fock_hbm, density_hbm, probe_ref, out_ref,
    fock, density, high, low, base,
    send1, recv1, gather1, turned, flat, recv2, gather2, send3, recv3, moved, gather4,
    fock_sem, density_sem, own_sem,
    s1, r1, s2, r2, s3, r3, s4, r4, s5, r5, s6, r6, s7, r7,
):
    r = lax.axis_index("row")
    c = lax.axis_index("col")
    rows = fock.shape[1]
    cols = fock.shape[2]
    m = probe_ref.shape[2]
    s = rows // nc

    def at(block):
        return pl.ds(pl.multiple_of(block * s, s), s)

    def peer_to(me, d, n):
        return lax.rem(me + 1 + d, n)

    def peer_from(me, d, n):
        return lax.rem(me + 2 * n - 1 - d, n)

    def fock_load(d):
        block = peer_to(c, d, nc)
        return pltpu.make_async_copy(
            fock_hbm.at[:, at(block), :], fock.at[:, at(block), :], fock_sem.at[d]
        )

    def density_load(d):
        block = peer_from(c, lax.rem(d + nc - 1, nc), nc)
        return pltpu.make_async_copy(
            density_hbm.at[:, at(block), :], density.at[:, at(block), :], density_sem.at[d]
        )

    def each(n, body):
        def step(d, carry):
            body(d)
            return carry

        lax.fori_loop(0, n, step, 0)

    each(nc, lambda d: fock_load(d).start())
    each(nc, lambda d: density_load(d).start())

    mine = nc * r + c
    wanted = nr * c + r
    goal = (lax.rem(mine, nr), lax.div(mine, nr))
    stays = mine == wanted

    barrier = pltpu.get_barrier_semaphore()

    def greet(where):
        pl.semaphore_signal(barrier, inc=1, device_id=where, device_id_type=MESH)

    def greet_next(d):
        other = lax.rem(mine + 1 + d, nr * nc)
        greet((lax.div(other, nc), lax.rem(other, nc)))

    each(nr * nc - 1, greet_next)

    base[:, :m] = probe_ref[0]
    base[:, m:] = probe_ref[1]
    top, rest = split(base[...])
    high[...] = top
    low[...] = rest

    pl.semaphore_wait(barrier, nr * nc - 1)

    def col_copy(d, source, target, ssem, rsem):
        return pltpu.make_async_remote_copy(
            src_ref=source, dst_ref=target.at[d], send_sem=ssem.at[d], recv_sem=rsem.at[d],
            device_id=(r, peer_to(c, d, nc)), device_id_type=MESH,
        )

    def row_copy(d, source, target, ssem, rsem):
        return pltpu.make_async_remote_copy(
            src_ref=source, dst_ref=target.at[d], send_sem=ssem.at[d], recv_sem=rsem.at[d],
            device_id=(peer_to(r, d, nr), c), device_id_type=MESH,
        )

    def forward(block, factor):
        right = (high[...], low[...])
        one = dot3(split(fock[0, at(block), :]), right)
        two = dot3(split(fock[1, at(block), :]), right)
        real = one[:, :m] - two[:, m:]
        imag = one[:, m:] + two[:, :m]
        piece = nc * r + block
        weight = jnp.where(lax.div(piece, nr) == c, 1.0, 0.0).astype(jnp.float32)
        own = base[at(lax.rem(piece, nr)), :] * weight
        return own[:, :m] - factor * imag, own[:, m:] + factor * real

    def forward_reduce(factor, load, send, recv, ssem, rsem):
        def step(d):
            if load:
                fock_load(d).wait()
            real, imag = forward(peer_to(c, d, nc), factor)
            send[d, :, :m] = real
            send[d, :, m:] = imag
            col_copy(d, send.at[d], recv, ssem, rsem).start()

        each(nc - 1, step)
        if load:
            fock_load(nc - 1).wait()
        real, imag = forward(c, factor)
        recv[nc - 1, :, :m] = real
        recv[nc - 1, :, m:] = imag

        def take(d):
            col_copy(d, send.at[d], recv, ssem, rsem).wait_recv()
            recv[nc - 1] += recv[d]

        each(nc - 1, take)

    forward_reduce(time_step, True, send1, recv1, s1, r1)

    gather1[nc - 1] = recv1[nc - 1]
    each(nc - 1, lambda d: col_copy(d, gather1.at[nc - 1], gather1, s2, r2).start())

    def backward(slot, d):
        density_load(d).wait()
        block = peer_from(c, slot, nc)
        left = split(gather1[slot].T)
        one = dot3(left, split(density[0, at(block), :]))
        two = dot3(left, split(density[1, at(block), :]))
        return one[:m] + two[m:], one[m:] - two[:m]

    real, imag = backward(nc - 1, 0)
    turned[:m] = real
    turned[m:] = imag

    def gathered(d):
        col_copy(d, gather1.at[nc - 1], gather1, s2, r2).wait_recv()
        real, imag = backward(d, d + 1)
        turned[:m] += real
        turned[m:] += imag

    each(nc - 1, gathered)
    flat[...] = turned[...].T

    each(nr - 1, lambda d: row_copy(d, flat.at[at(peer_to(r, d, nr)), :], recv2, s3, r3).start())
    recv2[nr - 1] = flat[at(r), :]

    def take_row(d):
        row_copy(d, flat.at[at(peer_to(r, d, nr)), :], recv2, s3, r3).wait_recv()
        recv2[nr - 1] += recv2[d]

    each(nr - 1, take_row)

    gather2[nr - 1] = recv2[nr - 1]
    each(nr - 1, lambda d: row_copy(d, gather2.at[nr - 1], gather2, s4, r4).start())

    def place(slot):
        value = gather2[slot]
        where = at(peer_from(r, slot, nr))
        top, rest = split(value)
        base[where, :] = value
        high[where, :] = top
        low[where, :] = rest

    place(nr - 1)

    def take_vector(d):
        row_copy(d, gather2.at[nr - 1], gather2, s4, r4).wait_recv()
        place(d)

    each(nr - 1, take_vector)

    forward_reduce(-time_step, False, send3, recv3, s5, r5)

    moved[...] = recv3[nc - 1]

    def move():
        return pltpu.make_async_remote_copy(
            src_ref=moved, dst_ref=gather4.at[nr - 1], send_sem=s6.at[0], recv_sem=r6.at[0],
            device_id=goal, device_id_type=MESH,
        )

    def stay():
        return pltpu.make_async_copy(moved, gather4.at[nr - 1], own_sem.at[0])

    @pl.when(stays)
    def _():
        stay().start()
        stay().wait()

    @pl.when(jnp.logical_not(stays))
    def _():
        move().start()
        move().wait()

    each(nr - 1, lambda d: row_copy(d, gather4.at[nr - 1], gather4, s7, r7).start())

    def emit(slot):
        where = at(peer_from(r, slot, nr))
        out_ref[0, where, :] = gather4[slot, :, :m]
        out_ref[1, where, :] = gather4[slot, :, m:]

    emit(nr - 1)

    def take_out(d):
        row_copy(d, gather4.at[nr - 1], gather4, s7, r7).wait_recv()
        emit(d)

    each(nr - 1, take_out)

    def drain_col(d):
        col_copy(d, send1.at[d], recv1, s1, r1).wait_send()
        col_copy(d, gather1.at[nc - 1], gather1, s2, r2).wait_send()
        col_copy(d, send3.at[d], recv3, s5, r5).wait_send()

    def drain_row(d):
        row_copy(d, flat.at[at(peer_to(r, d, nr)), :], recv2, s3, r3).wait_send()
        row_copy(d, gather2.at[nr - 1], gather2, s4, r4).wait_send()
        row_copy(d, gather4.at[nr - 1], gather4, s7, r7).wait_send()

    each(nc - 1, drain_col)
    each(nr - 1, drain_row)


def solution(mesh):
    nr = mesh.shape["row"]
    nc = mesh.shape["col"]

    def shards(fock, density, probe):
        _, rows, cols = fock.shape
        m = probe.shape[2]
        s = rows // nc
        f32 = jnp.float32
        vmem = pltpu.VMEM
        sem = pltpu.SemaphoreType.DMA
        many, few = (nc, s, 2 * m), (nr, s, 2 * m)
        return pl.pallas_call(
            functools.partial(kernel, nr, nc),
            out_shape=jax.ShapeDtypeStruct(probe.shape, f32),
            in_specs=[
                pl.BlockSpec(memory_space=pl.ANY),
                pl.BlockSpec(memory_space=pl.ANY),
                pl.BlockSpec(memory_space=pltpu.VMEM),
            ],
            out_specs=pl.BlockSpec(memory_space=pltpu.VMEM),
            scratch_shapes=[
                vmem(fock.shape, f32),
                vmem(density.shape, f32),
                vmem((cols, 2 * m), jnp.bfloat16),
                vmem((cols, 2 * m), jnp.bfloat16),
                vmem((cols, 2 * m), f32),
                vmem(many, f32),
                vmem(many, f32),
                vmem(many, f32),
                vmem((2 * m, cols), f32),
                vmem((cols, 2 * m), f32),
                vmem(few, f32),
                vmem(few, f32),
                vmem(many, f32),
                vmem(many, f32),
                vmem((s, 2 * m), f32),
                vmem(few, f32),
                sem((nc,)),
                sem((nc,)),
                sem((1,)),
                *[sem((nc,))] * 14,
            ],
            compiler_params=pltpu.CompilerParams(
                collective_id=0, has_side_effects=True, vmem_limit_bytes=62 * 1024 * 1024
            ),
            name="propagate",
        )(fock, density, probe)

    return jax.shard_map(
        shards,
        mesh=mesh,
        in_specs=(P(None, "row", "col"), P(None, "row", "col"), P(None, "col", None)),
        out_specs=P(None, "col", None),
        check_vma=False,
    )
```

time: 490 us -> 201 us (0.41); the launches traced: 481 us -> 201 us
  waiting for transfers between devices: 323 us -> 0 us
  Pallas kernels: 0 us -> 199 us
  matrix products: 132 us -> 0 us
  between operations: 14.2 us -> 0.01 us
  other arithmetic: 12.1 us -> 0 us
    pallas_call x0 -> x1, Pallas kernels: none -> 199 us  [shards(): pl.pallas_call(functools.partial(kernel, nr, nc), out_shape=jax.ShapeDtyp...]
    reduce_scatter x2 -> x0, waiting for transfers between devices: 135 us -> none  [reduce_cols(): lax.psum_scatter(partial_value, 'col', scatter_dimension=1, tiled=True)]
    dot_general x12 -> x0, matrix products: 132 us -> none  [the longest x8 68.9 us: plain_dot(): jnp.dot(left, right, precision=lax.Precision.HIGHEST, preferred_element_t...]
    all_gather x2 -> x0, waiting for transfers between devices: 100 us -> none  [reduce_cols(): return lax.all_gather(share, 'col', axis=1, tiled=True)]
    psum x2 -> x0, waiting for transfers between devices: 87.4 us -> none  [broadcast(): return lax.psum(block, axis)]
  transfers between devices with their start and end apart: 6 -> 0, of which waited for: 6 -> 0; matrix products, arithmetic and copies ran while one was open for 0% -> 0% of each run, Pallas kernels for 0% -> 0%
where the time goes in v1:
time: 201 us
  Pallas kernels  199 us (99%)
  local copies, waits for them, and re-layouts  2.26 us (1%)
    pallas_call x1, Pallas kernels, shards(): pl.pallas_call(functools.partial(kernel, nr, nc), out_shape=jax.ShapeDtyp...  199 us

profile of v1, /device:TPU:15, one launch (start us, length us, event | category | flops | bytes accessed | tf_op | source)
XLA Modules:
  0.0 200.8 jit_solution(10310568586082138940)
XLA Ops:
  0.0 198.5 %propagate.1 = f32[2,1024,128]{2,1,0:T(8,128)} custom-call(f32[2,2048,1024]{2,1,0:T(8,128)} %fock_hbm.1, f32[2,2048,1024]{2,1,0:T(8,128)} %density_hbm.1, f32[2,1024,128]{2,1,0:T(8,128)} %probe_ref.1), custom_call_target="tpu_custom_call" | custom-call | tf_op jit(solution)/shard_map/propagate/pallas_call | solution.py:256
  198.5 2.3 %copy.5 = f32[2,1024,128]{2,1,0:T(8,128)} copy(f32[2,1024,128]{2,1,0:T(8,128)} %propagate.1) | data formatting | bytes 2097152

commit v2 on v1

--- a/solution.py
+++ b/solution.py
@@ -34,6 +34,20 @@
     cols = fock.shape[2]
     m = probe_ref.shape[2]
     s = rows // nc
+    half = nc // 2
+    side = lax.div(c, half)
+    spot = lax.rem(c, half)
+
+    def block_to(e):
+        return lax.rem(side + 1 + e // half, 2) * half + lax.rem(spot + 1 + e % half, half)
+
+    def block_from(e):
+        return lax.rem(side + 1 + e // half, 2) * half + lax.rem(spot + half - 1 - e % half, half)
+
+    def near(e):
+        return side * half + lax.rem(spot + 1 + e % half, half)
+
+    across = lax.rem(side + 1, 2) * half + spot
 
     def at(block):
         return pl.ds(pl.multiple_of(block * s, s), s)
@@ -45,13 +59,13 @@
         return lax.rem(me + 2 * n - 1 - d, n)
 
     def fock_load(d):
-        block = peer_to(c, d, nc)
+        block = block_to(d)
         return pltpu.make_async_copy(
             fock_hbm.at[:, at(block), :], fock.at[:, at(block), :], fock_sem.at[d]
         )
 
     def density_load(d):
-        block = peer_from(c, lax.rem(d + nc - 1, nc), nc)
+        block = block_from(d)
         return pltpu.make_async_copy(
             density_hbm.at[:, at(block), :], density.at[:, at(block), :], density_sem.at[d]
         )
@@ -64,7 +78,10 @@
         lax.fori_loop(0, n, step, 0)
 
     each(nc, lambda d: fock_load(d).start())
-    each(nc, lambda d: density_load(d).start())
+    density_load(nc - 1).start()
+    density_load(half - 1).start()
+    each(half - 1, lambda d: density_load(half + d).start())
+    each(half - 1, lambda d: density_load(d).start())
 
     mine = nc * r + c
     wanted = nr * c + r
@@ -90,10 +107,10 @@
 
     pl.semaphore_wait(barrier, nr * nc - 1)
 
-    def col_copy(d, source, target, ssem, rsem):
+    def col_copy(e, where, source, target, ssem, rsem):
         return pltpu.make_async_remote_copy(
-            src_ref=source, dst_ref=target.at[d], send_sem=ssem.at[d], recv_sem=rsem.at[d],
-            device_id=(r, peer_to(c, d, nc)), device_id_type=MESH,
+            src_ref=source, dst_ref=target.at[e], send_sem=ssem.at[e], recv_sem=rsem.at[e],
+            device_id=(r, where), device_id_type=MESH,
         )
 
     def row_copy(d, source, target, ssem, rsem):
@@ -114,51 +131,90 @@
         return own[:, :m] - factor * imag, own[:, m:] + factor * real
 
     def forward_reduce(factor, load, send, recv, ssem, rsem):
-        def step(d):
+        def product(e, target):
             if load:
-                fock_load(d).wait()
-            real, imag = forward(peer_to(c, d, nc), factor)
-            send[d, :, :m] = real
-            send[d, :, m:] = imag
-            col_copy(d, send.at[d], recv, ssem, rsem).start()
-
-        each(nc - 1, step)
-        if load:
-            fock_load(nc - 1).wait()
-        real, imag = forward(c, factor)
-        recv[nc - 1, :, :m] = real
-        recv[nc - 1, :, m:] = imag
-
-        def take(d):
-            col_copy(d, send.at[d], recv, ssem, rsem).wait_recv()
-            recv[nc - 1] += recv[d]
-
-        each(nc - 1, take)
-
-    forward_reduce(time_step, True, send1, recv1, s1, r1)
+                fock_load(e).wait()
+            real, imag = forward(block_to(e), factor)
+            target[e, :, :m] = real
+            target[e, :, m:] = imag
+
+        def partial_copy(e):
+            return col_copy(e, near(e), send.at[e], recv, ssem, rsem)
+
+        def sum_copy():
+            return col_copy(half - 1, across, recv.at[half - 1], send, ssem, rsem)
+
+        def step(e):
+            product(e, send)
+            partial_copy(e).start()
+
+        def take(e, total):
+            partial_copy(e).wait_recv()
+            recv[total] += recv[e]
+
+        each(half - 1, step)
+        product(half - 1, recv)
+        each(half - 1, lambda d: step(half + d))
+        product(nc - 1, recv)
+        each(half - 1, lambda d: take(d, half - 1))
+        sum_copy().start()
+        each(half - 1, lambda d: take(half + d, nc - 1))
+        sum_copy().wait_recv()
+        recv[nc - 1] += send[half - 1]
+
+        def drain():
+            each(half - 1, lambda d: partial_copy(d).wait_send())
+            each(half - 1, lambda d: partial_copy(half + d).wait_send())
+            sum_copy().wait_send()
+
+        return drain
+
+    drain1 = forward_reduce(time_step, True, send1, recv1, s1, r1)
 
     gather1[nc - 1] = recv1[nc - 1]
-    each(nc - 1, lambda d: col_copy(d, gather1.at[nc - 1], gather1, s2, r2).start())
-
-    def backward(slot, d):
-        density_load(d).wait()
-        block = peer_from(c, slot, nc)
-        left = split(gather1[slot].T)
+    def across_copy():
+        return col_copy(half - 1, across, gather1.at[nc - 1], gather1, s2, r2)
+
+    def near_copy(d):
+        return col_copy(half + d, near(d), gather1.at[nc - 1], gather1, s2, r2)
+
+    def forward_copy(d):
+        return col_copy(d, near(d), gather1.at[half - 1], gather1, s2, r2)
+
+    across_copy().start()
+    each(half - 1, lambda d: near_copy(d).start())
+
+    def backward(e):
+        density_load(e).wait()
+        block = block_from(e)
+        left = split(gather1[e].T)
         one = dot3(left, split(density[0, at(block), :]))
         two = dot3(left, split(density[1, at(block), :]))
         return one[:m] + two[m:], one[m:] - two[:m]
 
-    real, imag = backward(nc - 1, 0)
+    real, imag = backward(nc - 1)
     turned[:m] = real
     turned[m:] = imag
 
-    def gathered(d):
-        col_copy(d, gather1.at[nc - 1], gather1, s2, r2).wait_recv()
-        real, imag = backward(d, d + 1)
+    across_copy().wait_recv()
+    each(half - 1, lambda d: forward_copy(d).start())
+
+    def add_backward(e):
+        real, imag = backward(e)
         turned[:m] += real
         turned[m:] += imag
 
-    each(nc - 1, gathered)
+    def gathered_near(d):
+        near_copy(d).wait_recv()
+        add_backward(half + d)
+
+    def gathered_far(d):
+        forward_copy(d).wait_recv()
+        add_backward(d)
+
+    add_backward(half - 1)
+    each(half - 1, gathered_near)
+    each(half - 1, gathered_far)
     flat[...] = turned[...].T
 
     each(nr - 1, lambda d: row_copy(d, flat.at[at(peer_to(r, d, nr)), :], recv2, s3, r3).start())
@@ -189,7 +245,7 @@
 
     each(nr - 1, take_vector)
 
-    forward_reduce(-time_step, False, send3, recv3, s5, r5)
+    drain3 = forward_reduce(-time_step, False, send3, recv3, s5, r5)
 
     moved[...] = recv3[nc - 1]
 
@@ -227,17 +283,17 @@
 
     each(nr - 1, take_out)
 
-    def drain_col(d):
-        col_copy(d, send1.at[d], recv1, s1, r1).wait_send()
-        col_copy(d, gather1.at[nc - 1], gather1, s2, r2).wait_send()
-        col_copy(d, send3.at[d], recv3, s5, r5).wait_send()
+    drain1()
+    drain3()
+    across_copy().wait_send()
+    each(half - 1, lambda d: near_copy(d).wait_send())
+    each(half - 1, lambda d: forward_copy(d).wait_send())
 
     def drain_row(d):
         row_copy(d, flat.at[at(peer_to(r, d, nr)), :], recv2, s3, r3).wait_send()
         row_copy(d, gather2.at[nr - 1], gather2, s4, r4).wait_send()
         row_copy(d, gather4.at[nr - 1], gather4, s7, r7).wait_send()
 
-    each(nc - 1, drain_col)
     each(nr - 1, drain_row)
 
 

time: 201 us -> 150 us (0.75)
  Pallas kernels: 199 us -> 147 us
    pallas_call x1, Pallas kernels: 199 us -> 147 us  [shards(): pl.pallas_call(functools.partial(kernel, nr, nc), out_shape=jax.ShapeDtyp...]
where the time goes in v2:
time: 150 us
  Pallas kernels  147 us (98%)
  local copies, waits for them, and re-layouts  2.26 us (2%)
    pallas_call x1, Pallas kernels, shards(): pl.pallas_call(functools.partial(kernel, nr, nc), out_shape=jax.ShapeDtyp...  147 us

profile of v2, /device:TPU:15, one launch (start us, length us, event | category | flops | bytes accessed | tf_op | source)
XLA Modules:
  0.0 149.7 jit_solution(16175481446192699773)
XLA Ops:
  0.0 147.4 %propagate.1 = f32[2,1024,128]{2,1,0:T(8,128)} custom-call(f32[2,2048,1024]{2,1,0:T(8,128)} %fock_hbm.1, f32[2,2048,1024]{2,1,0:T(8,128)} %density_hbm.1, f32[2,1024,128]{2,1,0:T(8,128)} %probe_ref.1), custom_call_target="tpu_custom_call" | custom-call | tf_op jit(solution)/shard_map/propagate/pallas_call | solution.py:312
  147.4 2.3 %copy.5 = f32[2,1024,128]{2,1,0:T(8,128)} copy(f32[2,1024,128]{2,1,0:T(8,128)} %propagate.1) | data formatting | bytes 2097152
